TPU v7x, 512 devices: a whole 4x4x16 slice. The times are simulated.
512 devices in a mesh: sec: 32 (over z, core), tile: 16 (over x, y).
Axes of the slice: x: 4, y: 4, z: 16, core: 2. Of those that a mesh axis runs over, the one named last changes fastest.
Arguments:
- left_env: bfloat16 [32, 14, 64, 128, 128], P('sec', None, 'tile'), may hold values from -0.5 to 0.5
- right_env: bfloat16 [32, 14, 64, 128, 128], P('sec', None, 'tile'), may hold values from -0.125 to 0.125
- edge_left: bfloat16 [32, 64, 128, 128], P('sec', 'tile'), may hold values from -0.5 to 0.5
- edge_right: bfloat16 [32, 64, 128, 128], P('sec', 'tile'), may hold values from -0.5 to 0.5
- inverse_sv: float32 [32, 64, 128], P('sec', 'tile'), may hold values from 1 to 10
- basis: int32 [32, 64, 128], P('sec', 'tile'), may hold values from 0 to 127, as said below
- lengths: int32 [32, 64], P('sec'), may hold values from 1 to 128, as said below
- partner: int32 [32, 14, 64], P('sec', None, 'tile'), may hold values from 0 to 63, each once within a row
- energy_left: float32 [32, 64, 128], P('sec', 'tile'), may hold values from 0.5 to 2.5
- energy_right: float32 [32, 64, 128], P('sec', 'tile'), may hold values from 0.5 to 2.5
Outputs:
- guess: bfloat16 [32, 64, 128, 128], P('sec', 'tile')
- lanczos_last: bfloat16 [32, 64, 128, 128], P('sec', 'tile')
- tridiag: float32 [32, 8], P('sec')
Inputs may be any that keep to these rules, and one draw needn't show every extreme that they name: `lengths`: the 64 sector sizes of each bond sum to 4096; on every bond one sector holds exactly 128 states. `basis`: for a sector of n states, entries 0 to n - 1 are a permutation of 0 to n - 1, and entry a is a for a >= n. `partner`: each channel's row of a bond names every sector once.
All inputs are finite; a program needn't handle non-finite values.
Results may differ from a plain program's by a relative error of at most 0.035.
Values may be sent and summed in bfloat16 or wider, within the bound.
No kernel may reach another device: no remote copies, remote signals or barrier semaphores. Data moves between devices by JAX's collectives and lax.ppermute only.
A program may use at most 64 MiB of HBM per device.

v0:
```python
import jax
import jax.numpy as jnp
from jax import lax
from jax.sharding import PartitionSpec as P

ITERS = 4


EPSILON = 1e-06


def passed_along(value, axis, by):
    peers = lax.axis_size(axis)
    pairs = [(i, i + by) for i in range(peers) if 0 <= i + by < peers]
    return lax.ppermute(value, axis, pairs)


def on_device(
    left_env,
    right_env,
    edge_left,
    edge_right,
    inverse_sv,
    basis,
    lengths,
    partner,
    energy_left,
    energy_right,
):
    per_dev = edge_left.shape[1]
    block_size = edge_left.shape[2]
    tile_pos = lax.axis_index("tile")
    all_lengths = lengths[0]
    own_lengths = lax.dynamic_slice_in_dim(all_lengths, tile_pos * per_dev, per_dev, 0)
    slot_index = jnp.arange(block_size, dtype=jnp.int32)
    alive_cols = slot_index[None, :] < own_lengths[:, None]
    live_pair = alive_cols[:, :, None] & alive_cols[:, None, :]
    live_count = jnp.sum(all_lengths.astype(jnp.float32) ** 2)
    neighbour = passed_along(edge_right, "sec", -1)
    at_end = lax.axis_index("sec") == lax.axis_size("sec") - 1
    edge_next = jnp.where(at_end, edge_right, neighbour)[0]
    chosen = jnp.take_along_axis(edge_next, basis[0][:, :, None], axis=1)
    scaled_left = jnp.where(
        alive_cols[:, None, :], edge_left[0].astype(jnp.float32) * inverse_sv[0][:, None, :], 0.0
    ).astype(jnp.bfloat16)
    merged = jnp.einsum("sab,sbc->sac", scaled_left, chosen, preferred_element_type=jnp.float32)
    merged = jnp.where(live_pair, merged, 0.0)
    squares = lax.psum(jnp.sum(merged * merged), "tile")
    guess = (merged / jnp.sqrt(squares / live_count + EPSILON)).astype(jnp.bfloat16)
    energies = energy_left[0][:, :, None] + energy_right[0][:, None, :]
    routes = partner[0]
    left_blocks = left_env[0]
    right_blocks = right_env[0]
    alphas = []
    betas = []
    beta_now = jnp.float32(0.0)
    vector = guess
    previous = jnp.zeros_like(guess)
    for iteration in range(ITERS):
        whole_vector = lax.all_gather(vector, "tile", axis=0, tiled=True)
        fetched = whole_vector[routes]
        inner_part = jnp.einsum(
            "wsab,wsbc->wsac", left_blocks, fetched, preferred_element_type=jnp.float32
        ).astype(jnp.bfloat16)
        coupled = jnp.einsum(
            "wsac,wsdc->sad", inner_part, right_blocks, preferred_element_type=jnp.float32
        )
        image_own = jnp.where(
            live_pair, energies * vector.astype(jnp.float32) + coupled, 0.0
        ).astype(jnp.bfloat16)
        present = vector.astype(jnp.float32)
        imaged = image_own.astype(jnp.float32)
        former = previous.astype(jnp.float32)
        alpha_now = lax.psum(jnp.sum(present * imaged), "tile") / live_count
        residue = imaged - alpha_now * present - beta_now * former
        beta_next = jnp.sqrt(lax.psum(jnp.sum(residue * residue), "tile") / live_count + EPSILON)
        previous = vector
        vector = (residue / beta_next).astype(jnp.bfloat16)
        beta_now = beta_next
        alphas.append(alpha_now)
        betas.append(beta_now)
    tridiag = jnp.stack(alphas + betas)
    return (guess[None], vector[None], tridiag[None])


def solution(mesh):
    placed = (
        P("sec", None, "tile", None, None),
        P("sec", None, "tile", None, None),
        P("sec", "tile", None, None),
        P("sec", "tile", None, None),
        P("sec", "tile", None),
        P("sec", "tile", None),
        P("sec", None),
        P("sec", None, "tile"),
        P("sec", "tile", None),
        P("sec", "tile", None),
    )
    return jax.shard_map(
        on_device,
        mesh=mesh,
        in_specs=placed,
        out_specs=(P("sec", "tile", None, None), P("sec", "tile", None, None), P("sec", None)),
        check_vma=False,
    )
```

profile of v0, /device:TPU:480, one launch (start us, length us, event | category | flops | bytes accessed | tf_op | source)
XLA Modules:
  0.0 645.8 jit_solution(18374770275864898590)
XLA Ops:
  7.2 0.0 copy-start
  7.2 0.0 copy-start.7
  7.2 0.0 copy-start.6
  7.2 0.0 copy-start.5
  7.2 0.0 all-gather.5.cloned.1.call-start
  7.3 2.5 collective-permute-start
  9.8 0.7 fusion.253
  10.4 0.7 dynamic-slice_bitcast_fusion
  11.2 0.8 iota_compare_fusion
  11.9 1.3 multiply_reduce_fusion.5
  13.2 0.0 collective-permute-done
  13.2 3.2 gather_fusion.4
  16.4 0.0 copy-done.7
  16.4 0.0 copy-done.6
  16.5 1.1 multiply_reduce_fusion.4
  17.6 41.4 %psum.63 = f32[]{:T(128)} all-reduce(f32[]{:T(128)} %get-tuple-element.3), channel_id=1, replica_groups=mesh['sec'=32,'tile'=16] {'tile'}, use_global_device_ids=true, to_apply=%region_1.2 | all-reduce | flops 1 | bytes 8 | tf_op jit(solution)/shard_map/psum | solution.py:48
  60.3 0.7 divide_convert_fusion.4
  61.0 0.0 all-gather.5.cloned.1.call-update
  61.0 0.0 all-gather.7.cloned.1.call-start
  61.1 0.0 copy-done.5
  61.1 0.1 copy.23
  61.2 0.1 reshape.135
  61.3 0.0 copy-start.4
  61.3 0.0 copy-start.8
  61.3 0.0 copy-start.9
  61.3 53.5 %all-gather.5.cloned.1.call-done = bf16[64,128,128]{2,1,0:T(8,128)(2,1)} async-done(((bf16[4,128,128]{2,1,0:T(8,128)(2,1)}), bf16[64,128,128]{2,1,0:T(8,128)(2,1)}) %all-gather.5.cloned.1.call-update) | async-done | bytes 2097168 | tf_op jit(solution)/shard_map/all_gather | solution.py:60
  114.8 3.6 gather_fusion
  118.4 0.0 copy-done.4
  118.4 4.5 fusion.231
  123.0 38.7 %psum.64 = f32[]{:T(128)} all-reduce(f32[]{:T(128)} %get-tuple-element.5), channel_id=1, replica_groups=mesh['sec'=32,'tile'=16] {'tile'}, use_global_device_ids=true, to_apply=%region_4.5 | all-reduce | flops 1 | bytes 8 | tf_op jit(solution)/shard_map/psum | solution.py:74
  163.1 0.7 multiply_reduce_fusion.3
  163.7 36.1 %psum.65 = f32[]{:T(128)} all-reduce(f32[]{:T(128)} %multiply_reduce_fusion.3), channel_id=1, replica_groups=mesh['sec'=32,'tile'=16] {'tile'}, use_global_device_ids=true, to_apply=%region_6.7 | all-reduce | flops 1 | bytes 8 | tf_op jit(solution)/shard_map/psum | solution.py:76
  201.2 0.7 divide_convert_fusion.3
  201.9 0.0 all-gather.7.cloned.1.call-update
  201.9 0.0 copy-start.2
  201.9 0.0 all-gather.9.cloned.1.call-start
  202.0 58.2 %all-gather.7.cloned.1.call-done = bf16[64,128,128]{2,1,0:T(8,128)(2,1)} async-done(((bf16[4,128,128]{2,1,0:T(8,128)(2,1)}), bf16[64,128,128]{2,1,0:T(8,128)(2,1)}) %all-gather.7.cloned.1.call-update) | async-done | bytes 2097168 | tf_op jit(solution)/shard_map/all_gather | solution.py:60
  260.2 3.6 gather_fusion.1
  263.8 4.5 fusion.234
  268.4 38.7 %psum.66 = f32[]{:T(128)} all-reduce(f32[]{:T(128)} %get-tuple-element.7), channel_id=1, replica_groups=mesh['sec'=32,'tile'=16] {'tile'}, use_global_device_ids=true, to_apply=%region_8.9 | all-reduce | flops 1 | bytes 8 | tf_op jit(solution)/shard_map/psum | solution.py:74
  308.4 0.7 multiply_reduce_fusion.2
  309.1 36.1 %psum.67 = f32[]{:T(128)} all-reduce(f32[]{:T(128)} %multiply_reduce_fusion.2), channel_id=1, replica_groups=mesh['sec'=32,'tile'=16] {'tile'}, use_global_device_ids=true, to_apply=%region_10.11 | all-reduce | flops 1 | bytes 8 | tf_op jit(solution)/shard_map/psum | solution.py:76
  346.5 0.7 divide_convert_fusion.2
  347.3 0.0 all-gather.9.cloned.1.call-update
  347.3 0.0 copy-start.1
  347.3 0.0 all-gather.11.cloned.1.call-start
  347.3 58.2 %all-gather.9.cloned.1.call-done = bf16[64,128,128]{2,1,0:T(8,128)(2,1)} async-done(((bf16[4,128,128]{2,1,0:T(8,128)(2,1)}), bf16[64,128,128]{2,1,0:T(8,128)(2,1)}) %all-gather.9.cloned.1.call-update) | async-done | bytes 2097168 | tf_op jit(solution)/shard_map/all_gather | solution.py:60
  405.5 3.6 gather_fusion.2
  409.2 4.5 fusion.237
  413.7 38.7 %psum.68 = f32[]{:T(128)} all-reduce(f32[]{:T(128)} %get-tuple-element.9), channel_id=1, replica_groups=mesh['sec'=32,'tile'=16] {'tile'}, use_global_device_ids=true, to_apply=%region_12.13 | all-reduce | flops 1 | bytes 8 | tf_op jit(solution)/shard_map/psum | solution.py:74
  453.8 0.7 multiply_reduce_fusion.1
  454.5 36.1 %psum.69 = f32[]{:T(128)} all-reduce(f32[]{:T(128)} %multiply_reduce_fusion.1), channel_id=1, replica_groups=mesh['sec'=32,'tile'=16] {'tile'}, use_global_device_ids=true, to_apply=%region_14.15 | all-reduce | flops 1 | bytes 8 | tf_op jit(solution)/shard_map/psum | solution.py:76
  491.9 0.7 divide_convert_fusion.1
  492.6 0.0 all-gather.11.cloned.1.call-update
  492.7 0.0 copy-start.3
  492.7 58.2 %all-gather.11.cloned.1.call-done = bf16[64,128,128]{2,1,0:T(8,128)(2,1)} async-done(((bf16[4,128,128]{2,1,0:T(8,128)(2,1)}), bf16[64,128,128]{2,1,0:T(8,128)(2,1)}) %all-gather.11.cloned.1.call-update) | async-done | bytes 2097168 | tf_op jit(solution)/shard_map/all_gather | solution.py:60
  550.9 3.6 gather_fusion.3
  554.6 4.5 fusion.228
  559.1 38.7 %psum.70 = f32[]{:T(128)} all-reduce(f32[]{:T(128)} %get-tuple-element.11), channel_id=1, replica_groups=mesh['sec'=32,'tile'=16] {'tile'}, use_global_device_ids=true, to_apply=%region_16.17 | all-reduce | flops 1 | bytes 8 | tf_op jit(solution)/shard_map/psum | solution.py:74
  599.2 0.7 multiply_reduce_fusion
  599.8 0.7 fusion.272
  600.5 36.1 %psum.71 = f32[]{:T(128)} all-reduce(f32[]{:T(128)} %multiply_reduce_fusion), channel_id=1, replica_groups=mesh['sec'=32,'tile'=16] {'tile'}, use_global_device_ids=true, to_apply=%region_18.19 | all-reduce | flops 1 | bytes 8 | tf_op jit(solution)/shard_map/psum | solution.py:76
  638.0 0.7 fusion.246
  638.7 0.6 stack.35
  (9 shorter events, 0.0 us)
Async XLA Ops:
  7.2 111.3 %copy-start = (bf16[1,14,4,128,128]{4,3,2,1,0:T(8,128)(2,1)S(1)}, bf16[1,14,4,128,128]{4,3,2,1,0:T(8,128)(2,1)}, u32[]{:S(2)}) copy-start(bf16[1,14,4,128,128]{4,3,2,1,0:T(8,128)(2,1)} %param.11) | copy-start | bytes 5505028
  7.2 9.3 %copy-start.7 = (f32[1,4,128]{2,1,0:T(4,128)S(1)}, f32[1,4,128]{2,1,0:T(4,128)}, u32[]{:S(2)}) copy-start(f32[1,4,128]{2,1,0:T(4,128)} %param.14) | copy-start | bytes 6148
  7.2 9.3 %copy-start.6 = (bf16[1,4,128,128]{3,2,1,0:T(8,128)(2,1)S(1)}, bf16[1,4,128,128]{3,2,1,0:T(8,128)(2,1)}, u32[]{:S(2)}) copy-start(bf16[1,4,128,128]{3,2,1,0:T(8,128)(2,1)} %param.12) | copy-start | bytes 393220
  7.2 53.9 %copy-start.5 = (s32[1,14,4]{1,2,0:T(4,128)S(1)}, s32[1,14,4]{1,2,0:T(4,128)}, u32[]{:S(2)}) copy-start(s32[1,14,4]{1,2,0:T(4,128)} %param.17) | copy-start | bytes 676
  7.2 107.6 %all-gather.5.cloned.1.call-start = ((), (), s32[]{:S(2)}) async-start(), calls=%async_computation | async-start | bytes 2228224 | tf_op jit(solution)/shard_map/all_gather | solution.py:60
  7.3 6.0 collective-permute-start
  61.0 199.2 %all-gather.7.cloned.1.call-start = ((), (), s32[]{:S(2)}) async-start(), calls=%async_computation.1 | async-start | bytes 2228224 | tf_op jit(solution)/shard_map/all_gather | solution.py:60
  61.3 57.2 %copy-start.4 = (bf16[4,128,128]{2,1,0:T(8,128)(2,1)S(1)}, bf16[4,128,128]{2,1,0:T(8,128)(2,1)}, u32[]{:S(2)}) copy-start(bf16[4,128,128]{2,1,0:T(8,128)(2,1)} %divide_convert_fusion.4) | copy-start | bytes 393220
  61.3 57.1 %copy-start.8 = (f32[1,4,128]{2,1,0:T(4,128)S(1)}, f32[1,4,128]{2,1,0:T(4,128)}, u32[]{:S(2)}) copy-start(f32[1,4,128]{2,1,0:T(4,128)} %param.19) | copy-start | bytes 6148
  61.3 57.1 %copy-start.9 = (f32[1,4,128]{2,1,0:T(4,128)S(1)}, f32[1,4,128]{2,1,0:T(4,128)}, u32[]{:S(2)}) copy-start(f32[1,4,128]{2,1,0:T(4,128)} %param.18) | copy-start | bytes 6148
  201.9 61.9 %copy-start.2 = (bf16[4,128,128]{2,1,0:T(8,128)(2,1)S(1)}, bf16[4,128,128]{2,1,0:T(8,128)(2,1)}, u32[]{:S(2)}) copy-start(bf16[4,128,128]{2,1,0:T(8,128)(2,1)} %divide_convert_fusion.3) | copy-start | bytes 393220
  201.9 203.6 %all-gather.9.cloned.1.call-start = ((), (), s32[]{:S(2)}) async-start(), calls=%async_computation.2 | async-start | bytes 2228224 | tf_op jit(solution)/shard_map/all_gather | solution.py:60
  347.3 61.9 %copy-start.1 = (bf16[4,128,128]{2,1,0:T(8,128)(2,1)S(1)}, bf16[4,128,128]{2,1,0:T(8,128)(2,1)}, u32[]{:S(2)}) copy-start(bf16[4,128,128]{2,1,0:T(8,128)(2,1)} %divide_convert_fusion.2) | copy-start | bytes 393220
  347.3 203.6 %all-gather.11.cloned.1.call-start = ((), (), s32[]{:S(2)}) async-start(), calls=%async_computation.3 | async-start | bytes 2228224 | tf_op jit(solution)/shard_map/all_gather | solution.py:60
  492.7 61.9 %copy-start.3 = (bf16[4,128,128]{2,1,0:T(8,128)(2,1)S(1)}, bf16[4,128,128]{2,1,0:T(8,128)(2,1)}, u32[]{:S(2)}) copy-start(bf16[4,128,128]{2,1,0:T(8,128)(2,1)} %divide_convert_fusion.1) | copy-start | bytes 393220
Sparse Core Ops, SparseCore 0:
  61.1 53.6 all-gather.4
  202.0 58.0 all-gather.6
  347.4 58.0 all-gather.8
  492.8 58.0 all-gather.10
where the time goes:
time: 652 us; the launch traced here: 646 us
  blocking collectives  341 us (52%)
  waiting for transfers between devices  228 us (35%)
  between operations  26.1 us (4%)
  local copies, waits for them, and re-layouts  19.3 us (3%)
  matrix products  19.3 us (3%)
  other arithmetic  9.72 us (1%)
    all_gather x4, waiting for transfers between devices, on_device(): whole_vector = lax.all_gather(vector, 'tile', axis=0, tiled=True)  228 us
    psum x4, blocking collectives, on_device(): alpha_now = lax.psum(jnp.sum(present * imaged), 'tile') / live_count  155 us
    psum x4, blocking collectives, on_device(): lax.psum(jnp.sum(residue * residue), 'tile') / live_count + EPSILON  144 us
    psum x1, blocking collectives, on_device(): squares = lax.psum(jnp.sum(merged * merged), 'tile')  41.4 us
    dot_general x4, matrix products, on_device(): jnp.einsum('wsac,wsdc->sad', inner_part, right_blocks, preferred_element_...  18.2 us
    gather x4, local copies, waits for them, and re-layouts, on_device(): fetched = whole_vector[routes]  14.6 us
  transfers between devices with their start and end apart: 5, of which 4 were waited for; matrix products, arithmetic and copies ran while one was open for 1% of the time, Pallas kernels for 0%

commit v1 on v0

v1 whole, which is shorter than its diff:
```python
import functools
import jax
import jax.numpy as jnp
from jax import lax
from jax.experimental import pallas as pl
from jax.experimental.pallas import tpu as pltpu
from jax.sharding import PartitionSpec as P

ITERS = 4
EPSILON = 1e-06
SIDE = 4
TAIL = 16
F32 = jnp.float32
BF16 = jnp.bfloat16
AXES = ("sec", "tile")


def passed_along(value, axis, by):
    peers = lax.axis_size(axis)
    pairs = [(i, i + by) for i in range(peers) if 0 <= i + by < peers]
    return lax.ppermute(value, axis, pairs)


def line_groups(n_sec, stage):
    rows = [[a * SIDE + b for b in range(SIDE)] for a in range(SIDE)]
    cols = [[a * SIDE + b for a in range(SIDE)] for b in range(SIDE)]
    groups = []
    for k in range(n_sec):
        for line in rows if (k % 2 == 0) == (stage == 0) else cols:
            groups.append([k * SIDE * SIDE + i for i in line])
    return groups


def gathered(copies, n_sec):
    rows = copies.shape[1]
    line = lax.all_to_all(copies, AXES, 0, 0, tiled=True, axis_index_groups=line_groups(n_sec, 0))
    line = jnp.broadcast_to(line.reshape(1, SIDE * rows, 128), (SIDE, SIDE * rows, 128))
    whole = lax.all_to_all(line, AXES, 0, 0, tiled=True, axis_index_groups=line_groups(n_sec, 1))
    return whole.reshape(SIDE * SIDE * rows, 128)


def place_of(owner, odd):
    high = owner // SIDE
    low = owner % SIDE
    return jnp.where(odd, low * SIDE + high, owner)


def lane_sums(block):
    return jnp.sum(block, axis=0, keepdims=True)


def in_pieces(sums):
    row = lax.broadcasted_iota(jnp.int32, (TAIL, 128), 0)
    out = jnp.zeros((TAIL, 128), F32)
    for q, value in enumerate(sums):
        for k in range(3):
            piece = value.astype(BF16).astype(F32)
            out = jnp.where(row == 3 * q + k, piece, out)
            value = value - piece
    return out.astype(BF16)


def totals(whole_ref, n_dev, rows, n_sums):
    acc = jnp.zeros((TAIL, 128), F32)
    for i in range(n_dev):
        acc = acc + whole_ref[i * rows + rows - TAIL : (i + 1) * rows, :].astype(F32)
    out = []
    for q in range(n_sums):
        lanes = jnp.sum(acc[3 * q : 3 * q + 3, :], axis=0, keepdims=True)
        out.append(jnp.sum(lanes, axis=1, keepdims=True))
    return out


def merge_body(per, lengths_s, lengths_v, own_edge, sent_edge, left, inv, basis, e_left, e_right,
               out_ref, energy_ref, merged_ref, state_ref):
    at_end = lax.axis_index("sec") == lax.axis_size("sec") - 1
    first = lax.axis_index("tile") * per
    row = lax.broadcasted_iota(jnp.int32, (128, 128), 0)
    col = lax.broadcasted_iota(jnp.int32, (128, 128), 1)
    squares = jnp.zeros((1, 128), F32)
    weighted = jnp.zeros((1, 128), F32)
    for s in range(per):
        n = lengths_s[0, first + s]
        live = (row < n) & (col < n)
        scaled = jnp.where(col < n, left[0, s].astype(F32) * inv[0, s : s + 1, :], 0.0).astype(BF16)
        pick = jnp.where(row == basis[0, s : s + 1, :], 1.0, 0.0).astype(BF16)
        moved = lax.dot_general(scaled, pick, (((1,), (1,)), ((), ())), preferred_element_type=F32)
        following = jnp.where(at_end, own_edge[0, s].astype(F32), sent_edge[0, s].astype(F32)).astype(BF16)
        merged = jnp.dot(moved.astype(BF16), following, preferred_element_type=F32)
        merged = jnp.where(live, merged, 0.0)
        e_rows = jnp.broadcast_to(e_left[0, s : s + 1, :], (128, 128)).T
        energy = jnp.where(live, e_rows + e_right[0, s : s + 1, :], 0.0)
        energy_ref[s] = energy
        merged_ref[s] = merged
        blocks = merged.astype(BF16)
        for k in range(SIDE):
            out_ref[k, s * 128 : (s + 1) * 128, :] = blocks
        square = merged * merged
        squares = squares + lane_sums(square)
        weighted = weighted + lane_sums(square * energy)
    tail = in_pieces([squares, weighted])
    for k in range(SIDE):
        out_ref[k, per * 128 : per * 128 + TAIL, :] = tail
    sizes = lengths_v[...].astype(F32)
    count = jnp.sum(sizes * sizes, axis=1, keepdims=True)
    state_ref[...] = jnp.zeros((16, 128), F32)
    state_ref[0:1, :] = jnp.broadcast_to(1.0 / count, (1, 128))


def coupled(per, n_w, s, whole, left, right, partner, odd, rows):
    def fetched(w):
        sector = partner[s, w]
        at = place_of(sector // per, odd) * rows + (sector % per) * 128
        return whole[pl.ds(pl.multiple_of(at, 16), 128), :]

    acc = jnp.zeros((128, 128), F32)
    for w in range(0, n_w, 2):
        inner = [
            jnp.dot(left[0, w + i, s], fetched(w + i), preferred_element_type=F32).astype(BF16)
            for i in range(2)
        ]
        acc = acc + lax.dot_general(
            jnp.concatenate(inner, axis=1),
            jnp.concatenate([right[0, w, s], right[0, w + 1, s]], axis=1),
            (((1,), (1,)), ((), ())),
            preferred_element_type=F32,
        )
    return acc


def step_body(step, per, n_w, n_dev, partner, whole, left, right, energy_ref, state_in, *refs):
    if step == 0:
        merged_ref, guess_ref, out_ref, vector_ref, image_ref, state_ref = refs
    elif step < ITERS - 1:
        v_prev, image_prev, out_ref, vector_ref, image_ref, state_ref = refs
    else:
        v_prev, image_prev, sums_ref, ahead_ref, vector_ref, state_ref = refs
    rows = per * 128 + TAIL
    odd = lax.axis_index("sec") % 2 == 1
    own = place_of(lax.axis_index("tile"), odd) * rows
    inv_count = state_in[0:1, 0:1]
    state = [state_in[k : k + 1, :] for k in range(16)]
    if step == 0:
        square, weighted = totals(whole, n_dev, rows, 2)
        over = 1.0 / jnp.sqrt(square * inv_count + EPSILON)
        shift = weighted * over * over * inv_count
    else:
        a, b, c, d = totals(whole, n_dev, rows, 4)
        alpha = a * inv_count
        late = alpha - state_in[1:2, 0:1]
        norm = jnp.maximum(b - 2.0 * late * c + late * late * d, 0.0)
        beta = jnp.sqrt(norm * inv_count + EPSILON)
        over = 1.0 / beta
        shift = alpha
        state[1 + step] = jnp.broadcast_to(alpha, (1, 128))
        state[5 + step] = jnp.broadcast_to(beta, (1, 128))
    state[1] = jnp.broadcast_to(shift, (1, 128))
    for k in range(16):
        state_ref[k : k + 1, :] = state[k]
    sums = [jnp.zeros((1, 128), F32) for _ in range(4)]
    for s in range(per):
        present = whole[pl.ds(pl.multiple_of(own + s * 128, 16), 128), :].astype(F32)
        energy = energy_ref[s]
        acc = coupled(per, n_w, s, whole, left, right, partner, odd, rows)
        image = jnp.where(energy > 0.0, energy * present + acc, 0.0)
        if step == 0:
            guess_ref[0, s] = (merged_ref[s] * over).astype(BF16)
            image = image * over
            vector = present * over
            ahead = image - shift * vector
        else:
            image = (image - late * image_prev[s]) * over
            vector = (present - late * v_prev[s]) * over
            ahead = image - shift * vector - beta * v_prev[s]
        sums[0] = sums[0] + lane_sums(vector * image)
        sums[1] = sums[1] + lane_sums(ahead * ahead)
        sums[2] = sums[2] + lane_sums(ahead * vector)
        sums[3] = sums[3] + lane_sums(vector * vector)
        vector_ref[s] = vector
        if step < ITERS - 1:
            image_ref[s] = image
            blocks = ahead.astype(BF16)
            for k in range(SIDE):
                out_ref[k, s * 128 : (s + 1) * 128, :] = blocks
        else:
            ahead_ref[s] = ahead
    if step < ITERS - 1:
        tail = in_pieces(sums)
        for k in range(SIDE):
            out_ref[k, per * 128 : per * 128 + TAIL, :] = tail
    else:
        for k in range(n_dev):
            for q in range(4):
                sums_ref[k, q : q + 1, :] = sums[q]
            sums_ref[k, 4:8, :] = jnp.zeros((4, 128), F32)


def last_body(per, n_dev, sums_ref, ahead_ref, v_prev, state_in, out_ref, tridiag_ref):
    acc = sums_ref[0]
    for k in range(1, n_dev):
        acc = acc + sums_ref[k]
    a, b, c, d = (jnp.sum(acc[q : q + 1, :], axis=1, keepdims=True) for q in range(4))
    inv_count = state_in[0:1, 0:1]
    alpha = a * inv_count
    late = alpha - state_in[1:2, 0:1]
    norm = jnp.maximum(b - 2.0 * late * c + late * late * d, 0.0)
    beta = jnp.sqrt(norm * inv_count + EPSILON)
    over = 1.0 / beta
    for s in range(per):
        out_ref[0, s] = ((ahead_ref[s] - late * v_prev[s]) * over).astype(BF16)
    lane = lax.broadcasted_iota(jnp.int32, (1, 128), 1)
    values = [state_in[2 + k : 3 + k, :] for k in range(3)] + [alpha]
    values += [state_in[6 + k : 7 + k, :] for k in range(3)] + [beta]
    line = jnp.zeros((1, 128), F32)
    for k, value in enumerate(values):
        line = jnp.where(lane == k, value, line)
    tridiag_ref[...] = line[:, :8]


def call(body, outs, n_smem, operands, name):
    vmem = pl.BlockSpec(memory_space=pltpu.VMEM)
    smem = pl.BlockSpec(memory_space=pltpu.SMEM)
    return pl.pallas_call(
        body,
        out_shape=[jax.ShapeDtypeStruct(shape, dtype) for shape, dtype in outs],
        in_specs=[smem] * n_smem + [vmem] * (len(operands) - n_smem),
        out_specs=[vmem] * len(outs),
        compiler_params=pltpu.CompilerParams(vmem_limit_bytes=24 << 20),
        name=name,
    )(*operands)


def on_device(
    n_sec,
    n_dev,
    left_env,
    right_env,
    edge_left,
    edge_right,
    inverse_sv,
    basis,
    lengths,
    partner,
    energy_left,
    energy_right,
):
    per = edge_left.shape[1]
    n_w = left_env.shape[1]
    rows = per * 128 + TAIL
    sent_edge = passed_along(edge_right, "sec", -1)
    routes = jnp.swapaxes(partner, 1, 2)[0]
    cube = ((per, 128, 128), F32)
    small = ((16, 128), F32)
    copies = ((SIDE, rows, 128), BF16)
    send, energy, merged, state = call(
        functools.partial(merge_body, per),
        [copies, cube, cube, small],
        1,
        (lengths, lengths, edge_right, sent_edge, edge_left, inverse_sv, basis, energy_left, energy_right),
        "merge",
    )
    for step in range(ITERS):
        whole = gathered(send, n_sec)
        body = functools.partial(step_body, step, per, n_w, n_dev)
        common = (routes, whole, left_env, right_env, energy, state)
        if step == 0:
            guess, send, vector, image, state = call(
                body,
                [((1, per, 128, 128), BF16), copies, cube, cube, small],
                1,
                common + (merged,),
                "step_first",
            )
        elif step < ITERS - 1:
            send, vector, image, state = call(
                body, [copies, cube, cube, small], 1, common + (vector, image), "step_next"
            )
        else:
            sums, ahead, vector, state = call(
                body,
                [((n_dev, 8, 128), F32), cube, cube, small],
                1,
                common + (vector, image),
                "step_last",
            )
    sums = lax.all_to_all(sums, "tile", 0, 0, tiled=True)
    last, tridiag = call(
        functools.partial(last_body, per, n_dev),
        [((1, per, 128, 128), BF16), ((1, 8), F32)],
        0,
        (sums, ahead, vector, state),
        "finish",
    )
    return guess, last, tridiag


def solution(mesh):
    placed = (
        P("sec", None, "tile", None, None),
        P("sec", None, "tile", None, None),
        P("sec", "tile", None, None),
        P("sec", "tile", None, None),
        P("sec", "tile", None),
        P("sec", "tile", None),
        P("sec", None),
        P("sec", None, "tile"),
        P("sec", "tile", None),
        P("sec", "tile", None),
    )
    return jax.shard_map(
        functools.partial(on_device, mesh.shape["sec"], mesh.shape["tile"]),
        mesh=mesh,
        in_specs=placed,
        out_specs=(P("sec", "tile", None, None), P("sec", "tile", None, None), P("sec", None)),
        check_vma=False,
    )
```

time: 652 us -> 163 us (0.25)
  waiting for transfers between devices: 228 us -> 2.82 us
  blocking collectives: 341 us -> 137 us
  between operations: 26.1 us -> 0.71 us
  matrix products: 19.3 us -> 0 us
  Pallas kernels: 0 us -> 13.3 us
  local copies, waits for them, and re-layouts: 19.3 us -> 6.32 us
  other arithmetic: 9.72 us -> 0 us
    psum x9 -> x0, blocking collectives: 341 us -> none  [the longest x4 155 us: on_device(): alpha_now = lax.psum(jnp.sum(present * imaged), 'tile') / live_count]
    all_gather x4 -> x0, waiting for transfers between devices: 228 us -> none  [on_device(): whole_vector = lax.all_gather(vector, 'tile', axis=0, tiled=True)]
    all_to_all x0 -> x9, blocking collectives: none -> 137 us  [the longest x4 79.5 us: gathered(): lax.all_to_all(line, AXES, 0, 0, tiled=True, axis_index_groups=line_group...]
    dot_general x5 -> x0, matrix products: 19.3 us -> none  [the longest x4 18.2 us: on_device(): jnp.einsum('wsac,wsdc->sad', inner_part, right_blocks, preferred_element_...]
    gather x5 -> x0, local copies, waits for them, and re-layouts: 17.7 us -> none  [the longest x4 14.6 us: on_device(): fetched = whole_vector[routes]]
    pallas_call x0 -> x6, Pallas kernels: none -> 13.3 us  [call(): pl.pallas_call(body, out_shape=[jax.ShapeDtypeStruct(shape, dtype) for sh...]
  transfers between devices with their start and end apart: 5 -> 1, of which waited for: 4 -> 1; matrix products, arithmetic and copies ran while one was open for 1% -> 0% of each run, Pallas kernels for 0% -> 0%
where the time goes in v1:
time: 163 us
  blocking collectives  137 us (84%)
  Pallas kernels  13.3 us (8%)
  local copies, waits for them, and re-layouts  6.32 us (4%)
  waiting for transfers between devices  2.82 us (2%)
  starting transfers between devices  2.35 us (1%)
    all_to_all x4, blocking collectives, gathered(): lax.all_to_all(line, AXES, 0, 0, tiled=True, axis_index_groups=line_group...  79.5 us
    all_to_all x4, blocking collectives, gathered(): lax.all_to_all(copies, AXES, 0, 0, tiled=True, axis_index_groups=line_gro...  47.5 us
    pallas_call x6, Pallas kernels, call(): pl.pallas_call(body, out_shape=[jax.ShapeDtypeStruct(shape, dtype) for sh...  13.3 us
    all_to_all x1, blocking collectives, on_device(): sums = lax.all_to_all(sums, 'tile', 0, 0, tiled=True)  10.3 us
    unnamed x20, local copies, waits for them, and re-layouts  5.21 us
  transfers between devices with their start and end apart: 1, of which 1 were waited for; matrix products, arithmetic and copies ran while one was open for 0% of the time, Pallas kernels for 0%

profile of v1, /device:TPU:480, one launch (start us, length us, event | category | flops | bytes accessed | tf_op | source)
XLA Modules:
  0.0 162.8 jit_solution(4695021440878349177)
XLA Ops:
  0.6 2.4 %collective-permute-start = (bf16[1,4,128,128]{3,2,1,0:T(8,128)(2,1)}, bf16[1,4,128,128]{3,2,1,0:T(8,128)(2,1)S(1)}, u32[]{:S(2)}, u32[]{:S(2)}) collective-permute-start(bf16[1,4,128,128]{3,2,1,0:T(8,128)(2,1)} %own_edge.1), channel_id=1, source_target_pairs={{16,0},{32,16},{48,32},{64,48},{80,64},{96,80},{112,96},{128,112},... | collective-permute-start | bytes 393224 | tf_op jit(solution)/shard_map/ppermute | solution.py:21
  3.0 2.8 %collective-permute-done.sent_edge = bf16[1,4,128,128]{3,2,1,0:T(8,128)(2,1)S(1)} collective-permute-done((bf16[1,4,128,128]{3,2,1,0:T(8,128)(2,1)}, bf16[1,4,128,128]{3,2,1,0:T(8,128)(2,1)S(1)}, u32[]{:S(2)}, u32[]{:S(2)}) %collective-permute-start) | collective-permute-done | bytes 131104 | tf_op jit(solution)/shard_map/ppermute | solution.py:21
  5.8 0.0 copy-start.2
  5.8 0.9 copy-done.2
  6.7 0.0 copy-start.3
  6.7 0.9 copy-done.3
  7.6 0.0 copy-start.5
  7.6 0.7 copy-done.5
  8.3 0.0 copy-start.6
  8.3 0.7 copy-done.6
  9.0 0.0 copy-start.7
  9.0 0.7 copy-done.7
  9.7 0.0 copy-start.8
  9.7 0.7 copy-done.8
  10.3 0.0 copy-start.9
  10.4 0.7 copy-done.9
  11.0 1.3 merge.1
  12.3 12.4 %all_to_all.45 = bf16[4,528,128]{2,1,0:T(8,128)(2,1)S(1)} all-to-all(bf16[4,528,128]{2,1,0:T(8,128)(2,1)S(1)} %get-tuple-element.26), channel_id=1, replica_groups={{0,1,2,3},{4,5,6,7},{8,9,10,11},{12,13,14,15},{16,20,24,28},{17,21,25,2..., dimensions={0} | all-to-all | bytes 1081344 | tf_op jit(solution)/shard_map/all_to_all | solution.py:36
  24.7 0.3 broadcast_in_dim.29
  25.0 0.0 copy-start
  25.0 0.0 copy-start.1
  25.1 0.0 copy-start.4
  25.1 21.2 %all_to_all.46 = bf16[4,2112,128]{2,1,0:T(8,128)(2,1)S(1)} all-to-all(bf16[4,2112,128]{2,1,0:T(8,128)(2,1)S(1)} %broadcast_in_dim.29), channel_id=1, replica_groups={{0,4,8,12},{1,5,9,13},{2,6,10,14},{3,7,11,15},{16,17,18,19},{20,21,22,2..., dimensions={0} | all-to-all | bytes 4325376 | tf_op jit(solution)/shard_map/all_to_all | solution.py:38
  46.3 0.0 copy-done
  46.3 0.0 copy-done.1
  46.3 0.0 copy-done.4
  46.3 3.2 %step_first.1 = (bf16[1,4,128,128]{3,2,1,0:T(8,128)(2,1)}, bf16[4,528,128]{2,1,0:T(8,128)(2,1)S(1)}, f32[4,128,128]{2,1,0:T(8,128)S(1)}, f32[4,128,128]{2,1,0:T(8,128)S(1)}, f32[16,128]{1,0:T(8,128)S(1)}) custom-call(s32[4,14]{1,0:T(4,128)S(1)} %bitcast.15, bf16[8448,128]{1,0:T(8,128)(2,1)S(1)} %bitcast.12, bf16[1,14,4,128,128]{4,3,2,1,0:T(8,128)(2,1)S(1)} %copy-done, ...), custom_call_target="tpu_custom_call" | custom-call | tf_op jit(solution)/shard_map/step_first/pallas_call | solution.py:223
  49.5 10.5 %all_to_all.47 = bf16[4,528,128]{2,1,0:T(8,128)(2,1)S(1)} all-to-all(bf16[4,528,128]{2,1,0:T(8,128)(2,1)S(1)} %get-tuple-element.31), channel_id=1, replica_groups={{0,1,2,3},{4,5,6,7},{8,9,10,11},{12,13,14,15},{16,20,24,28},{17,21,25,2..., dimensions={0} | all-to-all | bytes 1081344 | tf_op jit(solution)/shard_map/all_to_all | solution.py:36
  60.0 0.3 broadcast_in_dim.31
  60.3 19.3 %all_to_all.48 = bf16[4,2112,128]{2,1,0:T(8,128)(2,1)S(1)} all-to-all(bf16[4,2112,128]{2,1,0:T(8,128)(2,1)S(1)} %broadcast_in_dim.31), channel_id=1, replica_groups={{0,4,8,12},{1,5,9,13},{2,6,10,14},{3,7,11,15},{16,17,18,19},{20,21,22,2..., dimensions={0} | all-to-all | bytes 4325376 | tf_op jit(solution)/shard_map/all_to_all | solution.py:38
  79.6 2.7 %step_next.2 = (bf16[4,528,128]{2,1,0:T(8,128)(2,1)S(1)}, f32[4,128,128]{2,1,0:T(8,128)S(1)}, f32[4,128,128]{2,1,0:T(8,128)S(1)}, f32[16,128]{1,0:T(8,128)S(1)}) custom-call(s32[4,14]{1,0:T(4,128)S(1)} %bitcast.16, bf16[8448,128]{1,0:T(8,128)(2,1)S(1)} %bitcast.14, bf16[1,14,4,128,128]{4,3,2,1,0:T(8,128)(2,1)S(1)} %copy-done, ...), custom_call_target="tpu_custom_call" | custom-call | tf_op jit(solution)/shard_map/step_next/pallas_call | solution.py:223
  82.3 11.2 %all_to_all.49 = bf16[4,528,128]{2,1,0:T(8,128)(2,1)S(1)} all-to-all(bf16[4,528,128]{2,1,0:T(8,128)(2,1)S(1)} %get-tuple-element.35), channel_id=1, replica_groups={{0,1,2,3},{4,5,6,7},{8,9,10,11},{12,13,14,15},{16,20,24,28},{17,21,25,2..., dimensions={0} | all-to-all | bytes 1081344 | tf_op jit(solution)/shard_map/all_to_all | solution.py:36
  93.5 0.3 broadcast_in_dim.33
  93.7 19.3 %all_to_all.50 = bf16[4,2112,128]{2,1,0:T(8,128)(2,1)S(1)} all-to-all(bf16[4,2112,128]{2,1,0:T(8,128)(2,1)S(1)} %broadcast_in_dim.33), channel_id=1, replica_groups={{0,4,8,12},{1,5,9,13},{2,6,10,14},{3,7,11,15},{16,17,18,19},{20,21,22,2..., dimensions={0} | all-to-all | bytes 4325376 | tf_op jit(solution)/shard_map/all_to_all | solution.py:38
  113.1 2.7 %step_next.3 = (bf16[4,528,128]{2,1,0:T(8,128)(2,1)S(1)}, f32[4,128,128]{2,1,0:T(8,128)S(1)}, f32[4,128,128]{2,1,0:T(8,128)S(1)}, f32[16,128]{1,0:T(8,128)S(1)}) custom-call(s32[4,14]{1,0:T(4,128)S(1)} %bitcast.17, bf16[8448,128]{1,0:T(8,128)(2,1)S(1)} %bitcast.13, bf16[1,14,4,128,128]{4,3,2,1,0:T(8,128)(2,1)S(1)} %copy-done, ...), custom_call_target="tpu_custom_call" | custom-call | tf_op jit(solution)/shard_map/step_next/pallas_call | solution.py:223
  115.7 13.3 %all_to_all.51 = bf16[4,528,128]{2,1,0:T(8,128)(2,1)S(1)} all-to-all(bf16[4,528,128]{2,1,0:T(8,128)(2,1)S(1)} %get-tuple-element.39), channel_id=1, replica_groups={{0,1,2,3},{4,5,6,7},{8,9,10,11},{12,13,14,15},{16,20,24,28},{17,21,25,2..., dimensions={0} | all-to-all | bytes 1081344 | tf_op jit(solution)/shard_map/all_to_all | solution.py:36
  129.0 0.3 broadcast_in_dim.35
  129.3 19.7 %all_to_all.52 = bf16[4,2112,128]{2,1,0:T(8,128)(2,1)S(1)} all-to-all(bf16[4,2112,128]{2,1,0:T(8,128)(2,1)S(1)} %broadcast_in_dim.35), channel_id=1, replica_groups={{0,4,8,12},{1,5,9,13},{2,6,10,14},{3,7,11,15},{16,17,18,19},{20,21,22,2..., dimensions={0} | all-to-all | bytes 4325376 | tf_op jit(solution)/shard_map/all_to_all | solution.py:38
  149.0 2.7 %step_last.1 = (f32[16,8,128]{2,1,0:T(8,128)S(1)}, f32[4,128,128]{2,1,0:T(8,128)S(1)}, f32[4,128,128]{2,1,0:T(8,128)S(1)}, f32[16,128]{1,0:T(8,128)S(1)}) custom-call(s32[4,14]{1,0:T(4,128)S(1)} %bitcast.18, bf16[8448,128]{1,0:T(8,128)(2,1)S(1)} %bitcast.11, bf16[1,14,4,128,128]{4,3,2,1,0:T(8,128)(2,1)S(1)} %copy-done, ...), custom_call_target="tpu_custom_call" | custom-call | tf_op jit(solution)/shard_map/step_last/pallas_call | solution.py:223
  151.7 10.3 %all_to_all.53.sums_ref = f32[16,8,128]{2,1,0:T(8,128)S(1)} all-to-all(f32[16,8,128]{2,1,0:T(8,128)S(1)} %get-tuple-element.43), channel_id=1, replica_groups=mesh['sec'=32,'tile'=16] {'tile'}, dimensions={0} | all-to-all | bytes 131072 | tf_op jit(solution)/shard_map/all_to_all | solution.py:286
  161.9 0.8 finish.1
Async XLA Ops:
  0.6 5.2 %collective-permute-start = (bf16[1,4,128,128]{3,2,1,0:T(8,128)(2,1)}, bf16[1,4,128,128]{3,2,1,0:T(8,128)(2,1)S(1)}, u32[]{:S(2)}, u32[]{:S(2)}) collective-permute-start(bf16[1,4,128,128]{3,2,1,0:T(8,128)(2,1)} %own_edge.1), channel_id=1, source_target_pairs={{16,0},{32,16},{48,32},{64,48},{80,64},{96,80},{112,96},{128,112},... | collective-permute-start | bytes 393224 | tf_op jit(solution)/shard_map/ppermute | solution.py:21
  5.8 0.9 copy-start.2
  6.7 0.9 copy-start.3
  7.6 0.7 copy-start.5
  8.3 0.7 copy-start.6
  9.0 0.7 copy-start.7
  9.7 0.7 copy-start.8
  10.3 0.7 copy-start.9
  25.0 21.3 %copy-start = (bf16[1,14,4,128,128]{4,3,2,1,0:T(8,128)(2,1)S(1)}, bf16[1,14,4,128,128]{4,3,2,1,0:T(8,128)(2,1)}, u32[]{:S(2)}) copy-start(bf16[1,14,4,128,128]{4,3,2,1,0:T(8,128)(2,1)} %left.9) | copy-start | bytes 5505028
  25.0 21.2 %copy-start.1 = (bf16[1,14,4,128,128]{4,3,2,1,0:T(8,128)(2,1)S(1)}, bf16[1,14,4,128,128]{4,3,2,1,0:T(8,128)(2,1)}, u32[]{:S(2)}) copy-start(bf16[1,14,4,128,128]{4,3,2,1,0:T(8,128)(2,1)} %right.7) | copy-start | bytes 5505028
  25.1 21.2 %copy-start.4 = (s32[1,14,4]{1,2,0:T(4,128)S(1)}, s32[1,14,4]{1,2,0:T(4,128)}, u32[]{:S(2)}) copy-start(s32[1,14,4]{1,2,0:T(4,128)} %param.17) | copy-start | bytes 676

commit v2 on v1

--- a/solution.py
+++ b/solution.py
@@ -71,26 +71,56 @@
     return out
 
 
-def merge_body(per, lengths_s, lengths_v, own_edge, sent_edge, left, inv, basis, e_left, e_right,
-               out_ref, energy_ref, merged_ref, state_ref):
-    at_end = lax.axis_index("sec") == lax.axis_size("sec") - 1
+def prepare_body(per, n_w, lengths, partner, own_edge, left, inv, basis, e_left, e_right,
+                 moved_ref, own_ref, energy_ref, state_ref, places_ref,
+                 lengths_s, partner_s, lengths_v, left_v, inv_v, basis_v, e_left_v, e_right_v, sems):
+    pairs = [
+        (lengths, lengths_s),
+        (partner, partner_s),
+        (lengths, lengths_v),
+        (basis, basis_v),
+        (inv, inv_v),
+        (e_left, e_left_v),
+        (e_right, e_right_v),
+        (left, left_v),
+        (own_edge, own_ref),
+    ]
+    copies = [pltpu.make_async_copy(src, dst, sems.at[k]) for k, (src, dst) in enumerate(pairs)]
+    for copy in copies:
+        copy.start()
+    for copy in copies:
+        copy.wait()
+    rows = per * 128 + TAIL
+    odd = lax.axis_index("sec") % 2 == 1
+    for s in range(per):
+        for w in range(n_w):
+            sector = partner_s[s, w]
+            places_ref[s, w] = place_of(sector // per, odd) * rows + (sector % per) * 128
     first = lax.axis_index("tile") * per
     row = lax.broadcasted_iota(jnp.int32, (128, 128), 0)
     col = lax.broadcasted_iota(jnp.int32, (128, 128), 1)
+    for s in range(per):
+        n = lengths_s[0, first + s]
+        scaled = jnp.where(col < n, left_v[0, s].astype(F32) * inv_v[0, s : s + 1, :], 0.0).astype(BF16)
+        pick = jnp.where(row == basis_v[0, s : s + 1, :], 1.0, 0.0).astype(BF16)
+        moved = lax.dot_general(scaled, pick, (((1,), (1,)), ((), ())), preferred_element_type=F32)
+        moved_ref[s] = moved.astype(BF16)
+        e_rows = jnp.broadcast_to(e_left_v[0, s : s + 1, :], (128, 128)).T
+        energy_ref[s] = jnp.where((row < n) & (col < n), e_rows + e_right_v[0, s : s + 1, :], 0.0)
+    sizes = lengths_v[...].astype(F32)
+    count = jnp.sum(sizes * sizes, axis=1, keepdims=True)
+    state_ref[...] = jnp.broadcast_to(1.0 / count, (16, 128))
+
+
+def merge_body(per, sent_edge, own_edge, moved_ref, energy_ref, out_ref, merged_ref):
+    at_end = lax.axis_index("sec") == lax.axis_size("sec") - 1
     squares = jnp.zeros((1, 128), F32)
     weighted = jnp.zeros((1, 128), F32)
     for s in range(per):
-        n = lengths_s[0, first + s]
-        live = (row < n) & (col < n)
-        scaled = jnp.where(col < n, left[0, s].astype(F32) * inv[0, s : s + 1, :], 0.0).astype(BF16)
-        pick = jnp.where(row == basis[0, s : s + 1, :], 1.0, 0.0).astype(BF16)
-        moved = lax.dot_general(scaled, pick, (((1,), (1,)), ((), ())), preferred_element_type=F32)
         following = jnp.where(at_end, own_edge[0, s].astype(F32), sent_edge[0, s].astype(F32)).astype(BF16)
-        merged = jnp.dot(moved.astype(BF16), following, preferred_element_type=F32)
-        merged = jnp.where(live, merged, 0.0)
-        e_rows = jnp.broadcast_to(e_left[0, s : s + 1, :], (128, 128)).T
-        energy = jnp.where(live, e_rows + e_right[0, s : s + 1, :], 0.0)
-        energy_ref[s] = energy
+        energy = energy_ref[s]
+        merged = jnp.dot(moved_ref[s], following, preferred_element_type=F32)
+        merged = jnp.where(energy > 0.0, merged, 0.0)
         merged_ref[s] = merged
         blocks = merged.astype(BF16)
         for k in range(SIDE):
@@ -101,17 +131,11 @@
     tail = in_pieces([squares, weighted])
     for k in range(SIDE):
         out_ref[k, per * 128 : per * 128 + TAIL, :] = tail
-    sizes = lengths_v[...].astype(F32)
-    count = jnp.sum(sizes * sizes, axis=1, keepdims=True)
-    state_ref[...] = jnp.zeros((16, 128), F32)
-    state_ref[0:1, :] = jnp.broadcast_to(1.0 / count, (1, 128))
-
-
-def coupled(per, n_w, s, whole, left, right, partner, odd, rows):
+
+
+def coupled(n_w, s, whole, left, right, places):
     def fetched(w):
-        sector = partner[s, w]
-        at = place_of(sector // per, odd) * rows + (sector % per) * 128
-        return whole[pl.ds(pl.multiple_of(at, 16), 128), :]
+        return whole[pl.ds(pl.multiple_of(places[s, w], 16), 128), :]
 
     acc = jnp.zeros((128, 128), F32)
     for w in range(0, n_w, 2):
@@ -128,9 +152,9 @@
     return acc
 
 
-def step_body(step, per, n_w, n_dev, partner, whole, left, right, energy_ref, state_in, *refs):
+def step_body(step, per, n_w, n_dev, places, whole, left, right, energy_ref, state_in, *refs):
     if step == 0:
-        merged_ref, guess_ref, out_ref, vector_ref, image_ref, state_ref = refs
+        merged_ref, guess_ref, out_ref, vector_ref, image_ref, state_ref, guess_v, guess_sem = refs
     elif step < ITERS - 1:
         v_prev, image_prev, out_ref, vector_ref, image_ref, state_ref = refs
     else:
@@ -144,6 +168,10 @@
         square, weighted = totals(whole, n_dev, rows, 2)
         over = 1.0 / jnp.sqrt(square * inv_count + EPSILON)
         shift = weighted * over * over * inv_count
+        for s in range(per):
+            guess_v[0, s] = (merged_ref[s] * over).astype(BF16)
+        guess_copy = pltpu.make_async_copy(guess_v, guess_ref, guess_sem)
+        guess_copy.start()
     else:
         a, b, c, d = totals(whole, n_dev, rows, 4)
         alpha = a * inv_count
@@ -161,10 +189,9 @@
     for s in range(per):
         present = whole[pl.ds(pl.multiple_of(own + s * 128, 16), 128), :].astype(F32)
         energy = energy_ref[s]
-        acc = coupled(per, n_w, s, whole, left, right, partner, odd, rows)
+        acc = coupled(n_w, s, whole, left, right, places)
         image = jnp.where(energy > 0.0, energy * present + acc, 0.0)
         if step == 0:
-            guess_ref[0, s] = (merged_ref[s] * over).astype(BF16)
             image = image * over
             vector = present * over
             ahead = image - shift * vector
@@ -193,6 +220,8 @@
             for q in range(4):
                 sums_ref[k, q : q + 1, :] = sums[q]
             sums_ref[k, 4:8, :] = jnp.zeros((4, 128), F32)
+    if step == 0:
+        guess_copy.wait()
 
 
 def last_body(per, n_dev, sums_ref, ahead_ref, v_prev, state_in, out_ref, tridiag_ref):
@@ -217,17 +246,21 @@
     tridiag_ref[...] = line[:, :8]
 
 
-def call(body, outs, n_smem, operands, name):
-    vmem = pl.BlockSpec(memory_space=pltpu.VMEM)
-    smem = pl.BlockSpec(memory_space=pltpu.SMEM)
+VMEM = pl.BlockSpec(memory_space=pltpu.VMEM)
+SMEM = pl.BlockSpec(memory_space=pltpu.SMEM)
+HBM = pl.BlockSpec(memory_space=pltpu.HBM)
+
+
+def call(body, outs, operands, name, scratch=()):
     return pl.pallas_call(
         body,
-        out_shape=[jax.ShapeDtypeStruct(shape, dtype) for shape, dtype in outs],
-        in_specs=[smem] * n_smem + [vmem] * (len(operands) - n_smem),
-        out_specs=[vmem] * len(outs),
+        out_shape=[jax.ShapeDtypeStruct(shape, dtype) for _, shape, dtype in outs],
+        in_specs=[spec for spec, _ in operands],
+        out_specs=[spec for spec, _, _ in outs],
+        scratch_shapes=list(scratch),
         compiler_params=pltpu.CompilerParams(vmem_limit_bytes=24 << 20),
         name=name,
-    )(*operands)
+    )(*[array for _, array in operands])
 
 
 def on_device(
@@ -247,48 +280,69 @@
     per = edge_left.shape[1]
     n_w = left_env.shape[1]
     rows = per * 128 + TAIL
+    cube = (VMEM, (per, 128, 128), F32)
+    small = (VMEM, (16, 128), F32)
+    copies = (VMEM, (SIDE, rows, 128), BF16)
+    edge = (1, per, 128, 128)
     sent_edge = passed_along(edge_right, "sec", -1)
     routes = jnp.swapaxes(partner, 1, 2)[0]
-    cube = ((per, 128, 128), F32)
-    small = ((16, 128), F32)
-    copies = ((SIDE, rows, 128), BF16)
-    send, energy, merged, state = call(
+    given = (lengths, routes, edge_right, edge_left, inverse_sv, basis, energy_left, energy_right)
+    line = (1, per, 128)
+    moved, own_edge, energy, state, places = call(
+        functools.partial(prepare_body, per, n_w),
+        [(VMEM, (per, 128, 128), BF16), (VMEM, edge, BF16), cube, small, (SMEM, (per, n_w), jnp.int32)],
+        [(HBM, pltpu.with_memory_space_constraint(array, pltpu.HBM)) for array in given],
+        "prepare",
+        [
+            pltpu.SMEM(lengths.shape, jnp.int32),
+            pltpu.SMEM((per, n_w), jnp.int32),
+            pltpu.VMEM(lengths.shape, jnp.int32),
+            pltpu.VMEM(edge, BF16),
+            pltpu.VMEM(line, F32),
+            pltpu.VMEM(line, jnp.int32),
+            pltpu.VMEM(line, F32),
+            pltpu.VMEM(line, F32),
+            pltpu.SemaphoreType.DMA((9,)),
+        ],
+    )
+    send, merged = call(
         functools.partial(merge_body, per),
-        [copies, cube, cube, small],
-        1,
-        (lengths, lengths, edge_right, sent_edge, edge_left, inverse_sv, basis, energy_left, energy_right),
+        [copies, cube],
+        [(VMEM, sent_edge), (VMEM, own_edge), (VMEM, moved), (VMEM, energy)],
         "merge",
     )
     for step in range(ITERS):
         whole = gathered(send, n_sec)
         body = functools.partial(step_body, step, per, n_w, n_dev)
-        common = (routes, whole, left_env, right_env, energy, state)
+        common = [(SMEM, places)]
+        common += [(VMEM, array) for array in (whole, left_env, right_env, energy, state)]
         if step == 0:
             guess, send, vector, image, state = call(
                 body,
-                [((1, per, 128, 128), BF16), copies, cube, cube, small],
-                1,
-                common + (merged,),
+                [(HBM, edge, BF16), copies, cube, cube, small],
+                common + [(VMEM, merged)],
                 "step_first",
+                [pltpu.VMEM(edge, BF16), pltpu.SemaphoreType.DMA],
             )
         elif step < ITERS - 1:
             send, vector, image, state = call(
-                body, [copies, cube, cube, small], 1, common + (vector, image), "step_next"
+                body,
+                [copies, cube, cube, small],
+                common + [(VMEM, vector), (VMEM, image)],
+                "step_next",
             )
         else:
             sums, ahead, vector, state = call(
                 body,
-                [((n_dev, 8, 128), F32), cube, cube, small],
-                1,
-                common + (vector, image),
+                [(VMEM, (n_dev, 8, 128), F32), cube, cube, small],
+                common + [(VMEM, vector), (VMEM, image)],
                 "step_last",
             )
     sums = lax.all_to_all(sums, "tile", 0, 0, tiled=True)
     last, tridiag = call(
         functools.partial(last_body, per, n_dev),
-        [((1, per, 128, 128), BF16), ((1, 8), F32)],
-        0,
-        (sums, ahead, vector, state),
+        [(VMEM, edge, BF16), (VMEM, (1, 8), F32)],
+        [(VMEM, array) for array in (sums, ahead, vector, state)],
         "finish",
     )
     return guess, last, tridiag

time: 163 us -> 155 us (0.951)
  local copies, waits for them, and re-layouts: 6.32 us -> 1.13 us
  waiting for transfers between devices: 2.82 us -> 0.25 us
  blocking collectives: 137 us -> 135 us
    unnamed x20 -> x4, local copies, waits for them, and re-layouts: 5.21 us -> 0.01 us
    ppermute x1, waiting for transfers between devices: 2.82 us -> 0.25 us  [passed_along(): return lax.ppermute(value, axis, pairs)]
    all_to_all x4, blocking collectives: 47.5 us -> 45.4 us  [gathered(): lax.all_to_all(copies, AXES, 0, 0, tiled=True, axis_index_groups=line_gro...]
    pallas_call x6 -> x7, Pallas kernels: 13.3 us -> 14.6 us  [call(): pl.pallas_call(body, out_shape=[jax.ShapeDtypeStruct(shape, dtype) for _,...]
  transfers between devices with their start and end apart: 1 -> 1, of which waited for: 1 -> 1; matrix products, arithmetic and copies ran while one was open for 0% -> 0% of each run, Pallas kernels for 0% -> 2%
where the time goes in v2:
time: 155 us; the launch traced here: 154 us
  blocking collectives  135 us (87%)
  Pallas kernels  14.6 us (9%)
  starting transfers between devices  2.35 us (2%)
    all_to_all x4, blocking collectives, gathered(): lax.all_to_all(line, AXES, 0, 0, tiled=True, axis_index_groups=line_group...  79.2 us
    all_to_all x4, blocking collectives, gathered(): lax.all_to_all(copies, AXES, 0, 0, tiled=True, axis_index_groups=line_gro...  45.4 us
    pallas_call x7, Pallas kernels, call(): pl.pallas_call(body, out_shape=[jax.ShapeDtypeStruct(shape, dtype) for _,...  14.6 us
    all_to_all x1, blocking collectives, on_device(): sums = lax.all_to_all(sums, 'tile', 0, 0, tiled=True)  10.6 us
  transfers between devices with their start and end apart: 1, of which 1 were waited for; matrix products, arithmetic and copies ran while one was open for 0% of the time, Pallas kernels for 2%

profile of v2, /device:TPU:480, one launch (start us, length us, event | category | flops | bytes accessed | tf_op | source)
XLA Modules:
  0.0 154.3 jit_solution(14596769787544896244)
XLA Ops:
  0.6 2.4 %collective-permute-start = (bf16[1,4,128,128]{3,2,1,0:T(8,128)(2,1)}, bf16[1,4,128,128]{3,2,1,0:T(8,128)(2,1)S(1)}, u32[]{:S(2)}, u32[]{:S(2)}) collective-permute-start(bf16[1,4,128,128]{3,2,1,0:T(8,128)(2,1)} %own_edge.1), channel_id=1, source_target_pairs={{16,0},{32,16},{48,32},{64,48},{80,64},{96,80},{112,96},{128,112},... | collective-permute-start | bytes 393224 | tf_op jit(solution)/shard_map/ppermute | solution.py:21
  3.0 2.6 %prepare.1 = (bf16[4,128,128]{2,1,0:T(8,128)(2,1)S(1)}, bf16[1,4,128,128]{3,2,1,0:T(8,128)(2,1)S(1)}, f32[4,128,128]{2,1,0:T(8,128)S(1)}, f32[16,128]{1,0:T(8,128)S(1)}, s32[4,14]{1,0:T(4,128)S(1)}) custom-call(s32[1,64]{1,0:T(1,128)} %lengths.1, s32[4,14]{1,0:T(4,128)} %bitcast.19, bf16[1,4,128,128]{3,2,1,0:T(8,128)(2,1)} %own_edge.1, ...), custom_call_target="tpu_custom_call" | custom-call | tf_op jit(solution)/shard_map/prepare/pallas_call | solution.py:255
  5.6 0.2 collective-permute-done.sent_edge
  5.8 0.2 merge.1
  6.0 12.4 %all_to_all.45 = bf16[4,528,128]{2,1,0:T(8,128)(2,1)S(1)} all-to-all(bf16[4,528,128]{2,1,0:T(8,128)(2,1)S(1)} %get-tuple-element.33), channel_id=1, replica_groups={{0,1,2,3},{4,5,6,7},{8,9,10,11},{12,13,14,15},{16,20,24,28},{17,21,25,2..., dimensions={0} | all-to-all | bytes 1081344 | tf_op jit(solution)/shard_map/all_to_all | solution.py:36
  18.5 0.3 broadcast_in_dim.29
  18.8 0.0 copy-start
  18.8 0.0 copy-start.1
  18.8 21.2 %all_to_all.46 = bf16[4,2112,128]{2,1,0:T(8,128)(2,1)S(1)} all-to-all(bf16[4,2112,128]{2,1,0:T(8,128)(2,1)S(1)} %broadcast_in_dim.29), channel_id=1, replica_groups={{0,4,8,12},{1,5,9,13},{2,6,10,14},{3,7,11,15},{16,17,18,19},{20,21,22,2..., dimensions={0} | all-to-all | bytes 4325376 | tf_op jit(solution)/shard_map/all_to_all | solution.py:38
  40.0 0.0 copy-done
  40.0 0.0 copy-done.1
  40.0 3.2 %step_first.1 = (bf16[1,4,128,128]{3,2,1,0:T(8,128)(2,1)}, bf16[4,528,128]{2,1,0:T(8,128)(2,1)S(1)}, f32[4,128,128]{2,1,0:T(8,128)S(1)}, f32[4,128,128]{2,1,0:T(8,128)S(1)}, f32[16,128]{1,0:T(8,128)S(1)}) custom-call(s32[4,14]{1,0:T(4,128)S(1)} %get-tuple-element.29.places, bf16[8448,128]{1,0:T(8,128)(2,1)S(1)} %bitcast.12, ...), custom_call_target="tpu_custom_call" | custom-call | tf_op jit(solution)/shard_map/step_first/pallas_call | solution.py:255
  43.2 10.5 %all_to_all.47 = bf16[4,528,128]{2,1,0:T(8,128)(2,1)S(1)} all-to-all(bf16[4,528,128]{2,1,0:T(8,128)(2,1)S(1)} %get-tuple-element.37), channel_id=1, replica_groups={{0,1,2,3},{4,5,6,7},{8,9,10,11},{12,13,14,15},{16,20,24,28},{17,21,25,2..., dimensions={0} | all-to-all | bytes 1081344 | tf_op jit(solution)/shard_map/all_to_all | solution.py:36
  53.7 0.3 broadcast_in_dim.31
  54.0 19.3 %all_to_all.48 = bf16[4,2112,128]{2,1,0:T(8,128)(2,1)S(1)} all-to-all(bf16[4,2112,128]{2,1,0:T(8,128)(2,1)S(1)} %broadcast_in_dim.31), channel_id=1, replica_groups={{0,4,8,12},{1,5,9,13},{2,6,10,14},{3,7,11,15},{16,17,18,19},{20,21,22,2..., dimensions={0} | all-to-all | bytes 4325376 | tf_op jit(solution)/shard_map/all_to_all | solution.py:38
  73.3 2.6 %step_next.2 = (bf16[4,528,128]{2,1,0:T(8,128)(2,1)S(1)}, f32[4,128,128]{2,1,0:T(8,128)S(1)}, f32[4,128,128]{2,1,0:T(8,128)S(1)}, f32[16,128]{1,0:T(8,128)S(1)}) custom-call(s32[4,14]{1,0:T(4,128)S(1)} %get-tuple-element.29.places, bf16[8448,128]{1,0:T(8,128)(2,1)S(1)} %bitcast.14, bf16[1,14,4,128,128]{4,3,2,1,0:T(8,128)(2,1)S(1)} %copy-done, ...), custom_call_target="tpu_custom_call" | custom-call | tf_op jit(solution)/shard_map/step_next/pallas_call | solution.py:255
  75.9 10.5 %all_to_all.49 = bf16[4,528,128]{2,1,0:T(8,128)(2,1)S(1)} all-to-all(bf16[4,528,128]{2,1,0:T(8,128)(2,1)S(1)} %get-tuple-element.41), channel_id=1, replica_groups={{0,1,2,3},{4,5,6,7},{8,9,10,11},{12,13,14,15},{16,20,24,28},{17,21,25,2..., dimensions={0} | all-to-all | bytes 1081344 | tf_op jit(solution)/shard_map/all_to_all | solution.py:36
  86.5 0.3 broadcast_in_dim.33
  86.8 19.3 %all_to_all.50 = bf16[4,2112,128]{2,1,0:T(8,128)(2,1)S(1)} all-to-all(bf16[4,2112,128]{2,1,0:T(8,128)(2,1)S(1)} %broadcast_in_dim.33), channel_id=1, replica_groups={{0,4,8,12},{1,5,9,13},{2,6,10,14},{3,7,11,15},{16,17,18,19},{20,21,22,2..., dimensions={0} | all-to-all | bytes 4325376 | tf_op jit(solution)/shard_map/all_to_all | solution.py:38
  106.1 2.6 %step_next.3 = (bf16[4,528,128]{2,1,0:T(8,128)(2,1)S(1)}, f32[4,128,128]{2,1,0:T(8,128)S(1)}, f32[4,128,128]{2,1,0:T(8,128)S(1)}, f32[16,128]{1,0:T(8,128)S(1)}) custom-call(s32[4,14]{1,0:T(4,128)S(1)} %get-tuple-element.29.places, bf16[8448,128]{1,0:T(8,128)(2,1)S(1)} %bitcast.13, bf16[1,14,4,128,128]{4,3,2,1,0:T(8,128)(2,1)S(1)} %copy-done, ...), custom_call_target="tpu_custom_call" | custom-call | tf_op jit(solution)/shard_map/step_next/pallas_call | solution.py:255
  108.7 11.9 %all_to_all.51 = bf16[4,528,128]{2,1,0:T(8,128)(2,1)S(1)} all-to-all(bf16[4,528,128]{2,1,0:T(8,128)(2,1)S(1)} %get-tuple-element.45), channel_id=1, replica_groups={{0,1,2,3},{4,5,6,7},{8,9,10,11},{12,13,14,15},{16,20,24,28},{17,21,25,2..., dimensions={0} | all-to-all | bytes 1081344 | tf_op jit(solution)/shard_map/all_to_all | solution.py:36
  120.6 0.3 broadcast_in_dim.35
  120.9 19.3 %all_to_all.52 = bf16[4,2112,128]{2,1,0:T(8,128)(2,1)S(1)} all-to-all(bf16[4,2112,128]{2,1,0:T(8,128)(2,1)S(1)} %broadcast_in_dim.35), channel_id=1, replica_groups={{0,4,8,12},{1,5,9,13},{2,6,10,14},{3,7,11,15},{16,17,18,19},{20,21,22,2..., dimensions={0} | all-to-all | bytes 4325376 | tf_op jit(solution)/shard_map/all_to_all | solution.py:38
  140.2 2.6 %step_last.1 = (f32[16,8,128]{2,1,0:T(8,128)S(1)}, f32[4,128,128]{2,1,0:T(8,128)S(1)}, f32[4,128,128]{2,1,0:T(8,128)S(1)}, f32[16,128]{1,0:T(8,128)S(1)}) custom-call(s32[4,14]{1,0:T(4,128)S(1)} %get-tuple-element.29.places, bf16[8448,128]{1,0:T(8,128)(2,1)S(1)} %bitcast.11, bf16[1,14,4,128,128]{4,3,2,1,0:T(8,128)(2,1)S(1)} %copy-done, ...), custom_call_target="tpu_custom_call" | custom-call | tf_op jit(solution)/shard_map/step_last/pallas_call | solution.py:255
  142.8 10.6 %all_to_all.53.sums_ref = f32[16,8,128]{2,1,0:T(8,128)S(1)} all-to-all(f32[16,8,128]{2,1,0:T(8,128)S(1)} %get-tuple-element.49), channel_id=1, replica_groups=mesh['sec'=32,'tile'=16] {'tile'}, dimensions={0} | all-to-all | bytes 131072 | tf_op jit(solution)/shard_map/all_to_all | solution.py:341
  153.4 0.8 finish.1
Async XLA Ops:
  0.6 5.2 %collective-permute-start = (bf16[1,4,128,128]{3,2,1,0:T(8,128)(2,1)}, bf16[1,4,128,128]{3,2,1,0:T(8,128)(2,1)S(1)}, u32[]{:S(2)}, u32[]{:S(2)}) collective-permute-start(bf16[1,4,128,128]{3,2,1,0:T(8,128)(2,1)} %own_edge.1), channel_id=1, source_target_pairs={{16,0},{32,16},{48,32},{64,48},{80,64},{96,80},{112,96},{128,112},... | collective-permute-start | bytes 393224 | tf_op jit(solution)/shard_map/ppermute | solution.py:21
  18.8 21.2 %copy-start = (bf16[1,14,4,128,128]{4,3,2,1,0:T(8,128)(2,1)S(1)}, bf16[1,14,4,128,128]{4,3,2,1,0:T(8,128)(2,1)}, u32[]{:S(2)}) copy-start(bf16[1,14,4,128,128]{4,3,2,1,0:T(8,128)(2,1)} %left.9) | copy-start | bytes 5505028
  18.8 21.2 %copy-start.1 = (bf16[1,14,4,128,128]{4,3,2,1,0:T(8,128)(2,1)S(1)}, bf16[1,14,4,128,128]{4,3,2,1,0:T(8,128)(2,1)}, u32[]{:S(2)}) copy-start(bf16[1,14,4,128,128]{4,3,2,1,0:T(8,128)(2,1)} %right.7) | copy-start | bytes 5505028

commit v3 on v2

--- a/solution.py
+++ b/solution.py
@@ -137,24 +137,20 @@
     def fetched(w):
         return whole[pl.ds(pl.multiple_of(places[s, w], 16), 128), :]
 
-    acc = jnp.zeros((128, 128), F32)
-    for w in range(0, n_w, 2):
-        inner = [
-            jnp.dot(left[0, w + i, s], fetched(w + i), preferred_element_type=F32).astype(BF16)
-            for i in range(2)
-        ]
-        acc = acc + lax.dot_general(
-            jnp.concatenate(inner, axis=1),
-            jnp.concatenate([right[0, w, s], right[0, w + 1, s]], axis=1),
-            (((1,), (1,)), ((), ())),
-            preferred_element_type=F32,
-        )
-    return acc
+    inner = [
+        jnp.dot(left[0, w, s], fetched(w), preferred_element_type=F32).astype(BF16) for w in range(n_w)
+    ]
+    return lax.dot_general(
+        jnp.concatenate(inner, axis=1),
+        jnp.concatenate([right[0, w, s] for w in range(n_w)], axis=1),
+        (((1,), (1,)), ((), ())),
+        preferred_element_type=F32,
+    )
 
 
 def step_body(step, per, n_w, n_dev, places, whole, left, right, energy_ref, state_in, *refs):
     if step == 0:
-        merged_ref, guess_ref, out_ref, vector_ref, image_ref, state_ref, guess_v, guess_sem = refs
+        merged_ref, guess_ref, out_ref, vector_ref, image_ref, state_ref = refs
     elif step < ITERS - 1:
         v_prev, image_prev, out_ref, vector_ref, image_ref, state_ref = refs
     else:
@@ -169,9 +165,7 @@
         over = 1.0 / jnp.sqrt(square * inv_count + EPSILON)
         shift = weighted * over * over * inv_count
         for s in range(per):
-            guess_v[0, s] = (merged_ref[s] * over).astype(BF16)
-        guess_copy = pltpu.make_async_copy(guess_v, guess_ref, guess_sem)
-        guess_copy.start()
+            guess_ref[0, s] = (merged_ref[s] * over).astype(BF16)
     else:
         a, b, c, d = totals(whole, n_dev, rows, 4)
         alpha = a * inv_count
@@ -220,11 +214,12 @@
             for q in range(4):
                 sums_ref[k, q : q + 1, :] = sums[q]
             sums_ref[k, 4:8, :] = jnp.zeros((4, 128), F32)
-    if step == 0:
-        guess_copy.wait()
-
-
-def last_body(per, n_dev, sums_ref, ahead_ref, v_prev, state_in, out_ref, tridiag_ref):
+
+
+def last_body(per, n_dev, guess_v, sums_ref, ahead_ref, v_prev, state_in,
+              guess_ref, out_ref, tridiag_ref, sem):
+    guess_copy = pltpu.make_async_copy(guess_v, guess_ref, sem)
+    guess_copy.start()
     acc = sums_ref[0]
     for k in range(1, n_dev):
         acc = acc + sums_ref[k]
@@ -244,6 +239,7 @@
     for k, value in enumerate(values):
         line = jnp.where(lane == k, value, line)
     tridiag_ref[...] = line[:, :8]
+    guess_copy.wait()
 
 
 VMEM = pl.BlockSpec(memory_space=pltpu.VMEM)
@@ -319,10 +315,9 @@
         if step == 0:
             guess, send, vector, image, state = call(
                 body,
-                [(HBM, edge, BF16), copies, cube, cube, small],
+                [(VMEM, edge, BF16), copies, cube, cube, small],
                 common + [(VMEM, merged)],
                 "step_first",
-                [pltpu.VMEM(edge, BF16), pltpu.SemaphoreType.DMA],
             )
         elif step < ITERS - 1:
             send, vector, image, state = call(
@@ -339,11 +334,12 @@
                 "step_last",
             )
     sums = lax.all_to_all(sums, "tile", 0, 0, tiled=True)
-    last, tridiag = call(
+    guess, last, tridiag = call(
         functools.partial(last_body, per, n_dev),
-        [(VMEM, edge, BF16), (VMEM, (1, 8), F32)],
-        [(VMEM, array) for array in (sums, ahead, vector, state)],
+        [(HBM, edge, BF16), (VMEM, edge, BF16), (VMEM, (1, 8), F32)],
+        [(VMEM, array) for array in (guess, sums, ahead, vector, state)],
         "finish",
+        [pltpu.SemaphoreType.DMA],
     )
     return guess, last, tridiag
 

time: 155 us -> 152 us (0.981)
  Pallas kernels: 14.6 us -> 11.6 us
    pallas_call x7, Pallas kernels: 14.6 us -> 11.6 us  [call(): pl.pallas_call(body, out_shape=[jax.ShapeDtypeStruct(shape, dtype) for _,...]
where the time goes in v3:
time: 152 us; the launch traced here: 151 us
  blocking collectives  135 us (89%)
  Pallas kernels  11.6 us (8%)
  starting transfers between devices  2.35 us (2%)
    all_to_all x4, blocking collectives, gathered(): lax.all_to_all(line, AXES, 0, 0, tiled=True, axis_index_groups=line_group...  79.5 us
    all_to_all x4, blocking collectives, gathered(): lax.all_to_all(copies, AXES, 0, 0, tiled=True, axis_index_groups=line_gro...  45.4 us
    pallas_call x7, Pallas kernels, call(): pl.pallas_call(body, out_shape=[jax.ShapeDtypeStruct(shape, dtype) for _,...  11.6 us
    all_to_all x1, blocking collectives, on_device(): sums = lax.all_to_all(sums, 'tile', 0, 0, tiled=True)  10.3 us
  transfers between devices with their start and end apart: 1, of which 1 were waited for; matrix products, arithmetic and copies ran while one was open for 0% of the time, Pallas kernels for 2%

profile of v3, /device:TPU:480, one launch (start us, length us, event | category | flops | bytes accessed | tf_op | source)
XLA Modules:
  0.0 151.2 jit_solution(11049876967930232168)
XLA Ops:
  0.6 2.4 %collective-permute-start = (bf16[1,4,128,128]{3,2,1,0:T(8,128)(2,1)}, bf16[1,4,128,128]{3,2,1,0:T(8,128)(2,1)S(1)}, u32[]{:S(2)}, u32[]{:S(2)}) collective-permute-start(bf16[1,4,128,128]{3,2,1,0:T(8,128)(2,1)} %own_edge.1), channel_id=1, source_target_pairs={{16,0},{32,16},{48,32},{64,48},{80,64},{96,80},{112,96},{128,112},... | collective-permute-start | bytes 393224 | tf_op jit(solution)/shard_map/ppermute | solution.py:21
  3.0 2.6 %prepare.1 = (bf16[4,128,128]{2,1,0:T(8,128)(2,1)S(1)}, bf16[1,4,128,128]{3,2,1,0:T(8,128)(2,1)S(1)}, f32[4,128,128]{2,1,0:T(8,128)S(1)}, f32[16,128]{1,0:T(8,128)S(1)}, s32[4,14]{1,0:T(4,128)S(1)}) custom-call(s32[1,64]{1,0:T(1,128)} %lengths.1, s32[4,14]{1,0:T(4,128)} %bitcast.19, bf16[1,4,128,128]{3,2,1,0:T(8,128)(2,1)} %own_edge.1, ...), custom_call_target="tpu_custom_call" | custom-call | tf_op jit(solution)/shard_map/prepare/pallas_call | solution.py:251
  5.6 0.2 collective-permute-done.sent_edge
  5.8 0.2 merge.1
  6.0 12.4 %all_to_all.45 = bf16[4,528,128]{2,1,0:T(8,128)(2,1)S(1)} all-to-all(bf16[4,528,128]{2,1,0:T(8,128)(2,1)S(1)} %get-tuple-element.31), channel_id=1, replica_groups={{0,1,2,3},{4,5,6,7},{8,9,10,11},{12,13,14,15},{16,20,24,28},{17,21,25,2..., dimensions={0} | all-to-all | bytes 1081344 | tf_op jit(solution)/shard_map/all_to_all | solution.py:36
  18.5 0.3 broadcast_in_dim.29
  18.8 0.0 copy-start
  18.8 0.0 copy-start.1
  18.8 21.2 %all_to_all.46 = bf16[4,2112,128]{2,1,0:T(8,128)(2,1)S(1)} all-to-all(bf16[4,2112,128]{2,1,0:T(8,128)(2,1)S(1)} %broadcast_in_dim.29), channel_id=1, replica_groups={{0,4,8,12},{1,5,9,13},{2,6,10,14},{3,7,11,15},{16,17,18,19},{20,21,22,2..., dimensions={0} | all-to-all | bytes 4325376 | tf_op jit(solution)/shard_map/all_to_all | solution.py:38
  40.0 0.0 copy-done
  40.0 0.0 copy-done.1
  40.0 1.8 %step_first.1 = (bf16[1,4,128,128]{3,2,1,0:T(8,128)(2,1)S(1)}, bf16[4,528,128]{2,1,0:T(8,128)(2,1)S(1)}, f32[4,128,128]{2,1,0:T(8,128)S(1)}, f32[4,128,128]{2,1,0:T(8,128)S(1)}, f32[16,128]{1,0:T(8,128)S(1)}) custom-call(s32[4,14]{1,0:T(4,128)S(1)} %get-tuple-element.27.places, bf16[8448,128]{1,0:T(8,128)(2,1)S(1)} %bitcast.12, ...), custom_call_target="tpu_custom_call" | custom-call | tf_op jit(solution)/shard_map/step_first/pallas_call | solution.py:251
  41.9 10.5 %all_to_all.47 = bf16[4,528,128]{2,1,0:T(8,128)(2,1)S(1)} all-to-all(bf16[4,528,128]{2,1,0:T(8,128)(2,1)S(1)} %get-tuple-element.35), channel_id=1, replica_groups={{0,1,2,3},{4,5,6,7},{8,9,10,11},{12,13,14,15},{16,20,24,28},{17,21,25,2..., dimensions={0} | all-to-all | bytes 1081344 | tf_op jit(solution)/shard_map/all_to_all | solution.py:36
  52.4 0.3 broadcast_in_dim.31
  52.7 19.3 %all_to_all.48 = bf16[4,2112,128]{2,1,0:T(8,128)(2,1)S(1)} all-to-all(bf16[4,2112,128]{2,1,0:T(8,128)(2,1)S(1)} %broadcast_in_dim.31), channel_id=1, replica_groups={{0,4,8,12},{1,5,9,13},{2,6,10,14},{3,7,11,15},{16,17,18,19},{20,21,22,2..., dimensions={0} | all-to-all | bytes 4325376 | tf_op jit(solution)/shard_map/all_to_all | solution.py:38
  72.0 1.9 %step_next.2 = (bf16[4,528,128]{2,1,0:T(8,128)(2,1)S(1)}, f32[4,128,128]{2,1,0:T(8,128)S(1)}, f32[4,128,128]{2,1,0:T(8,128)S(1)}, f32[16,128]{1,0:T(8,128)S(1)}) custom-call(s32[4,14]{1,0:T(4,128)S(1)} %get-tuple-element.27.places, bf16[8448,128]{1,0:T(8,128)(2,1)S(1)} %bitcast.14, bf16[1,14,4,128,128]{4,3,2,1,0:T(8,128)(2,1)S(1)} %copy-done, ...), custom_call_target="tpu_custom_call" | custom-call | tf_op jit(solution)/shard_map/step_next/pallas_call | solution.py:251
  73.9 10.5 %all_to_all.49 = bf16[4,528,128]{2,1,0:T(8,128)(2,1)S(1)} all-to-all(bf16[4,528,128]{2,1,0:T(8,128)(2,1)S(1)} %get-tuple-element.39), channel_id=1, replica_groups={{0,1,2,3},{4,5,6,7},{8,9,10,11},{12,13,14,15},{16,20,24,28},{17,21,25,2..., dimensions={0} | all-to-all | bytes 1081344 | tf_op jit(solution)/shard_map/all_to_all | solution.py:36
  84.4 0.3 broadcast_in_dim.33
  84.7 19.3 %all_to_all.50 = bf16[4,2112,128]{2,1,0:T(8,128)(2,1)S(1)} all-to-all(bf16[4,2112,128]{2,1,0:T(8,128)(2,1)S(1)} %broadcast_in_dim.33), channel_id=1, replica_groups={{0,4,8,12},{1,5,9,13},{2,6,10,14},{3,7,11,15},{16,17,18,19},{20,21,22,2..., dimensions={0} | all-to-all | bytes 4325376 | tf_op jit(solution)/shard_map/all_to_all | solution.py:38
  104.0 1.9 %step_next.3 = (bf16[4,528,128]{2,1,0:T(8,128)(2,1)S(1)}, f32[4,128,128]{2,1,0:T(8,128)S(1)}, f32[4,128,128]{2,1,0:T(8,128)S(1)}, f32[16,128]{1,0:T(8,128)S(1)}) custom-call(s32[4,14]{1,0:T(4,128)S(1)} %get-tuple-element.27.places, bf16[8448,128]{1,0:T(8,128)(2,1)S(1)} %bitcast.13, bf16[1,14,4,128,128]{4,3,2,1,0:T(8,128)(2,1)S(1)} %copy-done, ...), custom_call_target="tpu_custom_call" | custom-call | tf_op jit(solution)/shard_map/step_next/pallas_call | solution.py:251
  105.9 11.9 %all_to_all.51 = bf16[4,528,128]{2,1,0:T(8,128)(2,1)S(1)} all-to-all(bf16[4,528,128]{2,1,0:T(8,128)(2,1)S(1)} %get-tuple-element.43), channel_id=1, replica_groups={{0,1,2,3},{4,5,6,7},{8,9,10,11},{12,13,14,15},{16,20,24,28},{17,21,25,2..., dimensions={0} | all-to-all | bytes 1081344 | tf_op jit(solution)/shard_map/all_to_all | solution.py:36
  117.8 0.3 broadcast_in_dim.35
  118.1 19.7 %all_to_all.52 = bf16[4,2112,128]{2,1,0:T(8,128)(2,1)S(1)} all-to-all(bf16[4,2112,128]{2,1,0:T(8,128)(2,1)S(1)} %broadcast_in_dim.35), channel_id=1, replica_groups={{0,4,8,12},{1,5,9,13},{2,6,10,14},{3,7,11,15},{16,17,18,19},{20,21,22,2..., dimensions={0} | all-to-all | bytes 4325376 | tf_op jit(solution)/shard_map/all_to_all | solution.py:38
  137.7 1.9 %step_last.1 = (f32[16,8,128]{2,1,0:T(8,128)S(1)}, f32[4,128,128]{2,1,0:T(8,128)S(1)}, f32[4,128,128]{2,1,0:T(8,128)S(1)}, f32[16,128]{1,0:T(8,128)S(1)}) custom-call(s32[4,14]{1,0:T(4,128)S(1)} %get-tuple-element.27.places, bf16[8448,128]{1,0:T(8,128)(2,1)S(1)} %bitcast.11, bf16[1,14,4,128,128]{4,3,2,1,0:T(8,128)(2,1)S(1)} %copy-done, ...), custom_call_target="tpu_custom_call" | custom-call | tf_op jit(solution)/shard_map/step_last/pallas_call | solution.py:251
  139.6 10.3 %all_to_all.53.sums_ref = f32[16,8,128]{2,1,0:T(8,128)S(1)} all-to-all(f32[16,8,128]{2,1,0:T(8,128)S(1)} %get-tuple-element.47), channel_id=1, replica_groups=mesh['sec'=32,'tile'=16] {'tile'}, dimensions={0} | all-to-all | bytes 131072 | tf_op jit(solution)/shard_map/all_to_all | solution.py:336
  149.9 1.3 finish.1
Async XLA Ops:
  0.6 5.2 %collective-permute-start = (bf16[1,4,128,128]{3,2,1,0:T(8,128)(2,1)}, bf16[1,4,128,128]{3,2,1,0:T(8,128)(2,1)S(1)}, u32[]{:S(2)}, u32[]{:S(2)}) collective-permute-start(bf16[1,4,128,128]{3,2,1,0:T(8,128)(2,1)} %own_edge.1), channel_id=1, source_target_pairs={{16,0},{32,16},{48,32},{64,48},{80,64},{96,80},{112,96},{128,112},... | collective-permute-start | bytes 393224 | tf_op jit(solution)/shard_map/ppermute | solution.py:21
  18.8 21.2 %copy-start = (bf16[1,14,4,128,128]{4,3,2,1,0:T(8,128)(2,1)S(1)}, bf16[1,14,4,128,128]{4,3,2,1,0:T(8,128)(2,1)}, u32[]{:S(2)}) copy-start(bf16[1,14,4,128,128]{4,3,2,1,0:T(8,128)(2,1)} %left.9) | copy-start | bytes 5505028
  18.8 21.2 %copy-start.1 = (bf16[1,14,4,128,128]{4,3,2,1,0:T(8,128)(2,1)S(1)}, bf16[1,14,4,128,128]{4,3,2,1,0:T(8,128)(2,1)}, u32[]{:S(2)}) copy-start(bf16[1,14,4,128,128]{4,3,2,1,0:T(8,128)(2,1)} %right.7) | copy-start | bytes 5505028
